TPU v7x, 32 devices: a whole 2x2x4 slice. The times are simulated.
32 devices in a mesh: groups: 2 (over x), gx: 16 (over z, y, core).
Axes of the slice: x: 2, y: 2, z: 4, core: 2. Of those that a mesh axis runs over, the one named last changes fastest.
Arguments:
- features: bfloat16 [64, 16, 64, 128], P(('groups', 'gx')), parts along dimension 0, may hold values from -6 to 6
- cotangent: bfloat16 [64, 16, 64, 128], P(('groups', 'gx')), parts along dimension 0, may hold values from -6 to 6
- wall_flags: int32 [64, 16, 128], P(('groups', 'gx')), parts along dimension 0, may hold values 0 or 1
- mode_counts: int32 [64], replicated, may hold values from 1 to 16, as said below
- offsets: int32 [6, 3], replicated, may hold values from -2 to 2, as said below
- point_weight: bfloat16 [64, 64], replicated, may hold values from -0.75 to 0.75
- kernel_weight: bfloat16 [6, 64, 64], replicated, may hold values from -0.3125 to 0.3125
- lap_weight: bfloat16 [64, 64], replicated, may hold values from -0.125 to 0.125
- spec_weight: bfloat16 [16, 64, 64], replicated, may hold values from -1 to 1
- bias: float32 [64], replicated, may hold values from -3 to 3
Outputs:
- input_grad: bfloat16 [64, 16, 64, 128], P(('groups', 'gx')), parts along dimension 0
- kernel_grad: float32 [12, 64, 64], P('groups'), parts along dimension 0
There are 2 independent parts, one for each index of `groups`. A program takes and returns all parts, laid end to end along the dimension named above; an argument that names none is the same for every part. Nothing has to cross between parts.
Inputs may be any that keep to these rules, and one draw needn't show every extreme that they name: Column 0 holds x offsets in -1..1 and both -1 and 1 occur; columns 1 and 2 hold y and z offsets in -2..2, and -2 and 2 occur in each of them. `mode_counts`: some channel keeps 16 modes and some channel keeps 1.
All inputs are finite; a program needn't handle non-finite values. No bound on the sum of `wall_flags` on one device may be relied on, other than what follows from the above.
Results may differ from a plain program's by a relative error of at most 0.0066.
Values may be sent and summed in bfloat16 or wider, within the bound.
A program may use at most 256 MiB of HBM per device.

v0:
```python
from functools import partial
import math
import jax
import jax.numpy as jnp
from jax import lax
from jax.sharding import PartitionSpec as P

RAD = 2


def with_halo(cells, sides, width):
    for axis, dim in sides:
        count = lax.axis_size(axis)
        ends = count - 1
        head = lax.slice_in_dim(cells, 0, width, axis=dim)
        tail = lax.slice_in_dim(cells, cells.shape[dim] - width, cells.shape[dim], axis=dim)
        cells = jnp.concatenate(
            [
                lax.ppermute(tail, axis, [(i, (i + 1) % count) for i in range(ends)]),
                cells,
                lax.ppermute(head, axis, [((i + 1) % count, i) for i in range(ends)]),
            ],
            axis=dim,
        )
    return cells


def basis_table(mode_total, length):
    mode_index = jnp.arange(mode_total, dtype=jnp.float32)[:, None]
    cell_index = jnp.arange(length, dtype=jnp.float32)[None, :]
    phase_angle = math.pi / (2.0 * length) * mode_index * (2.0 * cell_index + 1.0)
    amplitude = jnp.where(mode_index == 0.0, math.sqrt(1.0 / length), math.sqrt(2.0 / length))
    return (amplitude * jnp.cos(phase_angle)).astype(jnp.bfloat16)


def pencil_work(pencil, spec_weight, kept_modes, adjoint):
    basis = basis_table(spec_weight.shape[0], pencil.shape[0])
    coefficients = jnp.einsum(
        "kx,xycz->kycz", basis, pencil, preferred_element_type=jnp.float32
    ).astype(jnp.bfloat16)
    if adjoint:
        masked = coefficients * kept_modes[:, None, :, None].astype(jnp.bfloat16)
        mixed_modes = jnp.einsum(
            "koc,kyoz->kycz", spec_weight, masked, preferred_element_type=jnp.float32
        ).astype(jnp.bfloat16)
    else:
        mixed_modes = jnp.einsum(
            "koc,kycz->kyoz", spec_weight, coefficients, preferred_element_type=jnp.float32
        )
        mixed_modes = (mixed_modes * kept_modes[:, None, :, None]).astype(jnp.bfloat16)
    return jnp.einsum(
        "kx,kyoz->xyoz", basis, mixed_modes, preferred_element_type=jnp.float32
    ).astype(jnp.bfloat16)


def spectral(slab, spec_weight, kept_modes, adjoint):
    result = pencil_work(
        lax.all_to_all(slab, "gx", split_axis=1, concat_axis=0, tiled=True),
        spec_weight,
        kept_modes,
        adjoint,
    )
    return lax.all_to_all(result, "gx", split_axis=0, concat_axis=1, tiled=True)


def laplace_ext(extended):
    padded = jnp.pad(extended, ((0, 0), (1, 1), (0, 0), (1, 1))).astype(jnp.float32)
    centre_cells = padded[1:-1, 1:-1, :, 1:-1]
    neighbours = padded[2:, 1:-1, :, 1:-1] + padded[:-2, 1:-1, :, 1:-1]
    neighbours = neighbours + padded[1:-1, 2:, :, 1:-1] + padded[1:-1, :-2, :, 1:-1]
    neighbours = neighbours + padded[1:-1, 1:-1, :, 2:] + padded[1:-1, 1:-1, :, :-2]
    return (neighbours - 6.0 * centre_cells).astype(jnp.bfloat16)


def pad_sides(extended):
    return jnp.pad(extended, ((0, 0), (RAD, RAD), (0, 0), (RAD, RAD)))


def window_of(padded, offset, direction, slab_shape):
    starts = (
        1 + direction * offset[0],
        RAD + direction * offset[1],
        0,
        RAD + direction * offset[2],
    )
    return lax.dynamic_slice(padded, starts, slab_shape)


def gelu_slope(preact, upstream):
    _, pullback = jax.vjp(partial(jax.nn.gelu, approximate=True), preact)
    return pullback(upstream)[0]


def per_device(
    features,
    cotangent,
    wall_flags,
    mode_counts,
    offsets,
    point_weight,
    kernel_weight,
    lap_weight,
    spec_weight,
    bias,
):
    mode_total = spec_weight.shape[0]
    tile_total = kernel_weight.shape[0]
    kept_modes = (jnp.arange(mode_total, dtype=jnp.int32)[:, None] < mode_counts[None, :]).astype(
        jnp.float32
    )
    fluid_mask = (1 - wall_flags).astype(jnp.float32)[:, :, None, :]
    extended = with_halo(features, (("gx", 0),), 1)
    padded_field = pad_sides(extended)
    local_part = jnp.einsum(
        "oc,xycz->xyoz", point_weight, features, preferred_element_type=jnp.float32
    )
    local_part = local_part + jnp.einsum(
        "oc,xycz->xyoz", lap_weight, laplace_ext(extended), preferred_element_type=jnp.float32
    )
    for tile in range(tile_total):
        moved = window_of(padded_field, offsets[tile], 1, features.shape)
        local_part = local_part + jnp.einsum(
            "oc,xycz->xyoz", kernel_weight[tile], moved, preferred_element_type=jnp.float32
        )
    local_part = local_part + bias[:, None]
    spectral_part = spectral(features, spec_weight, kept_modes, False)
    preact = local_part + spectral_part.astype(jnp.float32)
    weighted = (gelu_slope(preact, cotangent.astype(jnp.float32)) * fluid_mask).astype(jnp.bfloat16)
    spec_grad = spectral(weighted, spec_weight, kept_modes, True)
    ext_grad = with_halo(weighted, (("gx", 0),), 1)
    padded_grad = pad_sides(ext_grad)
    input_grad = jnp.einsum(
        "oc,xyoz->xycz", point_weight, weighted, preferred_element_type=jnp.float32
    )
    input_grad = input_grad + jnp.einsum(
        "oc,xyoz->xycz", lap_weight, laplace_ext(ext_grad), preferred_element_type=jnp.float32
    )
    input_grad = input_grad + spec_grad.astype(jnp.float32)
    tile_grads = []
    for tile in range(tile_total):
        back_moved = window_of(padded_grad, offsets[tile], -1, weighted.shape)
        input_grad = input_grad + jnp.einsum(
            "oc,xyoz->xycz", kernel_weight[tile], back_moved, preferred_element_type=jnp.float32
        )
        tile_grads.append(
            jnp.einsum("xyoz,xycz->oc", back_moved, features, preferred_element_type=jnp.float32)
        )
    local_grad = jnp.stack(tile_grads, axis=0)
    scaling = float(
        lax.axis_size("gx") * features.shape[0] * features.shape[1] * features.shape[3]
    ) ** (-0.5)
    summed = lax.psum(local_grad, "gx")
    return (input_grad.astype(jnp.bfloat16), summed * scaling)


def solution(mesh):
    return jax.shard_map(
        per_device,
        mesh=mesh,
        in_specs=(
            P(("groups", "gx"), None, None, None),
            P(("groups", "gx"), None, None, None),
            P(("groups", "gx"), None, None),
            P(),
            P(),
            P(),
            P(),
            P(),
            P(),
            P(),
        ),
        out_specs=(P(("groups", "gx"), None, None, None), P("groups", None, None)),
        check_vma=False,
    )
```

profile of v0, /device:TPU:0, one launch (start us, length us, event | category | flops | bytes accessed | tf_op | source)
XLA Modules:
  0.0 241.2 jit_solution(13705008029308537028)
XLA Ops:
  8.4 2.4 collective-permute-start
  12.0 1.9 copy.40
  13.9 9.4 %all-to-all-start = ((bf16[2,16,64,128]{3,2,0,1:T(8,128)(2,1)}), bf16[2,16,64,128]{3,2,0,1:T(8,128)(2,1)S(1)}, u32[]{:S(2)}, u32[]{:S(2)}) async-start(bf16[2,16,64,128]{3,2,0,1:T(8,128)(2,1)} %copy.40), calls=%async_computation | async-start | bytes 1048576 | tf_op jit(solution)/shard_map/all_to_all | solution.py:58
  61.1 1.5 fusion.48
  67.4 6.0 %all-to-all-start.1 = ((bf16[32,1,64,128]{3,2,1,0:T(8,128)(2,1)}), bf16[32,1,64,128]{3,2,1,0:T(8,128)(2,1)S(1)}, u32[]{:S(2)}, u32[]{:S(2)}) async-start(bf16[32,1,64,128]{3,2,1,0:T(8,128)(2,1)} %copy.44), calls=%async_computation.1 | async-start | bytes 1048576 | tf_op jit(solution)/shard_map/all_to_all | solution.py:63
  74.2 1.4 fusion.50
  75.7 1.4 fusion.51
  77.1 2.9 %convolution_add_fusion.1 = f32[2,16,128,64]{2,3,1,0:T(8,128)} fusion(f32[2,16,128,64]{2,3,1,0:T(8,128)S(1)} %copy-done.3, f32[4,18,64,130]{3,2,1,0:T(8,128)S(1)} %pad_convert_fusion.1, bf16[64,64]{1,0:T(8,128)(2,1)S(1)} %copy-done.12), kind=kOutput, calls=%fused_computation.37 | convolution fusion | flops 35913728 | bytes 9453568 | tf_op jit(solution)/shard_map/oc,xycz->xyoz/dot_general | solution.py:117
  79.9 8.0 %all-to-all-done.1 = bf16[32,1,64,128]{3,2,1,0:T(8,128)(2,1)S(1)} async-done(((bf16[32,1,64,128]{3,2,1,0:T(8,128)(2,1)}), bf16[32,1,64,128]{3,2,1,0:T(8,128)(2,1)S(1)}, u32[]{:S(2)}, u32[]{:S(2)}) %all-to-all-start.1) | async-done | bytes 524320 | tf_op jit(solution)/shard_map/all_to_all | solution.py:63
  88.7 4.2 %fusion.33 = bf16[2,16,64,128]{3,2,1,0:T(8,128)(2,1)S(1)} fusion(bf16[2,16,64,128]{3,2,1,0:T(8,128)(2,1)} %param.11, f32[2,16,128,64]{2,3,1,0:T(8,128)} %fusion.51, f32[2,16,128,64]{2,3,1,0:T(8,128)} %fusion.50, f32[2,16,128,64]{2,3,1,0:T(8,128)} %fusion.49, f32[2,16,128,64]{2,3,1,0:T(8,128)} %fusion.48, f32[2,16,128,64]{2,3,1,0:T(8,128)S(1)} %fusion.47, ...), kind=kOutput, calls=%fused_computation.72 | convolution fusion | flops 41680896 | bytes 8946188 | tf_op jit(solution)/shard_map/oc,xycz->xyoz/dot_general | solution.py:122
  93.7 1.9 collective-permute-start.2
  97.0 6.9 %all-to-all-start.2 = ((bf16[2,16,64,128]{3,2,0,1:T(8,128)(2,1)}), bf16[2,16,64,128]{3,2,0,1:T(8,128)(2,1)}, u32[]{:S(2)}, u32[]{:S(2)}) async-start(bf16[2,16,64,128]{3,2,0,1:T(8,128)(2,1)} %copy.49), calls=%async_computation.2 | async-start | bytes 1048576 | tf_op jit(solution)/shard_map/all_to_all | solution.py:58
  110.9 1.5 convolution_bitcast_fusion.2
  112.3 1.4 convolution_bitcast_fusion.3
  113.7 4.7 %all-to-all-done.2 = bf16[2,16,64,128]{3,2,0,1:T(8,128)(2,1)} async-done(((bf16[2,16,64,128]{3,2,0,1:T(8,128)(2,1)}), bf16[2,16,64,128]{3,2,0,1:T(8,128)(2,1)}, u32[]{:S(2)}, u32[]{:S(2)}) %all-to-all-start.2) | async-done | bytes 524320 | tf_op jit(solution)/shard_map/all_to_all | solution.py:58
  118.4 1.5 fusion.22
  121.7 4.1 %all-to-all-start.3 = ((bf16[32,1,64,128]{3,2,1,0:T(8,128)(2,1)}), bf16[32,1,64,128]{3,2,1,0:T(8,128)(2,1)S(1)}, u32[]{:S(2)}, u32[]{:S(2)}) async-start(bf16[32,1,64,128]{3,2,1,0:T(8,128)(2,1)} %copy.55), calls=%async_computation.3 | async-start | bytes 1048576 | tf_op jit(solution)/shard_map/all_to_all | solution.py:63
  126.9 1.4 convolution_bitcast_fusion.4
  128.3 1.5 convolution_bitcast_fusion
  129.8 2.9 %pad_convert_fusion = f32[4,18,64,130]{3,2,1,0:T(8,128)} fusion(bf16[4,16,64,128]{3,2,1,0:T(8,128)(2,1)S(1)} %pad_maximum_fusion), kind=kLoop, calls=%fused_computation.12 | loop fusion | flops 599040 | bytes 3444736 | tf_op jit(solution)/shard_map/convert_element_type | solution.py:67
  132.7 89.0 %all-reduce.6.cloned.1.call-done = f32[6,64,64]{2,1,0:T(8,128)} async-done(((f32[6,64,64]{2,1,0:T(8,128)}), f32[6,64,64]{2,1,0:T(8,128)}) %all-reduce.6.cloned.1.call-update) | async-done | bytes 98320 | tf_op jit(solution)/shard_map/psum | solution.py:152
  221.7 1.6 broadcast_multiply_fusion
  223.4 7.5 %fusion.15 = f32[2,16,64,128]{3,2,1,0:T(8,128)S(1)} fusion(f32[2,16,128,64]{2,3,1,0:T(8,128)} %fusion.74, f32[4,18,64,130]{3,2,1,0:T(8,128)} %pad_convert_fusion, bf16[64,64]{1,0:T(8,128)(2,1)S(1)} %copy-done.13, bf16[16,2,1,64,128]{4,3,1,0,2:T(8,128)(2,1)S(1)} %bitcast.306), kind=kOutput, calls=%fused_computation.40 | convolution fusion | flops 36438016 | bytes 9969664 | tf_op jit(solution)/shard_map/oc,xyoz->xycz/dot_general | solution.py:135
  230.8 3.5 %fusion.16 = bf16[2,16,64,128]{3,2,1,0:T(8,128)(2,1)} fusion(f32[2,16,64,128]{3,2,1,0:T(8,128)} %convolution_bitcast_fusion, f32[2,16,64,128]{3,2,1,0:T(8,128)S(1)} %convolution_bitcast_fusion.1, f32[2,16,64,128]{3,2,1,0:T(8,128)} %convolution_bitcast_fusion.2, f32[2,16,64,128]{3,2,1,0:T(8,128)} %convolution_bitcast_fusion.3, ...), kind=kOutput, calls=%fused_computation.43 | convolution fusion | flops 35389440 | bytes 7880716 | tf_op jit(solution)/shard_map/oc,xyoz->xycz/dot_general | solution.py:142
  (70 shorter events, 24.5 us)
Async XLA Ops:
  7.2 57.9 %copy-start = (bf16[16,64,64]{2,1,0:T(8,128)(2,1)S(1)}, bf16[16,64,64]{2,1,0:T(8,128)(2,1)}, u32[]{:S(2)}) copy-start(bf16[16,64,64]{2,1,0:T(8,128)(2,1)} %param.18) | copy-start | bytes 393220
  7.2 16.2 %copy-start.1 = (bf16[2,16,64,128]{3,2,1,0:T(8,128)(2,1)S(1)}, bf16[2,16,64,128]{3,2,1,0:T(8,128)(2,1)}, u32[]{:S(2)}) copy-start(bf16[2,16,64,128]{3,2,1,0:T(8,128)(2,1)} %param.10) | copy-start | bytes 1572868
  7.2 16.2 %copy-start.11 = (s32[64]{0:T(128)S(1)}, s32[64]{0:T(128)}, u32[]{:S(2)}) copy-start(s32[64]{0:T(128)} %param.13) | copy-start | bytes 772
  7.2 16.2 %copy-start.5 = (bf16[64,64]{1,0:T(8,128)(2,1)S(1)}, bf16[64,64]{1,0:T(8,128)(2,1)}, u32[]{:S(2)}) copy-start(bf16[64,64]{1,0:T(8,128)(2,1)} %param.15) | copy-start | bytes 24580
  7.2 17.5 %copy-start.8 = (s32[2,16,128]{2,1,0:T(8,128)S(1)}, s32[2,16,128]{2,1,0:T(8,128)}, u32[]{:S(2)}) copy-start(s32[2,16,128]{2,1,0:T(8,128)} %param.12) | copy-start | bytes 49156
  7.2 17.5 %copy-start.6 = (s32[6,3]{0,1:T(4,128)S(1)}, s32[6,3]{0,1:T(4,128)}, u32[]{:S(2)}) copy-start(s32[6,3]{0,1:T(4,128)} %param.14) | copy-start | bytes 220
  8.4 52.2 %collective-permute-start = (bf16[1,16,64,128]{3,2,1,0:T(8,128)(2,1)S(1)}, bf16[1,16,64,128]{3,2,1,0:T(8,128)(2,1)S(1)}, u32[]{:S(2)}, u32[]{:S(2)}) collective-permute-start(bf16[1,16,64,128]{3,2,1,0:T(8,128)(2,1)S(1)} %get-tuple-element.5), channel_id=1, source_target_pairs={{0,1},{1,2},{2,3},{3,4},{4,5},{5,6},{6,7},{7,8},{8,9},{9,10},{10,1... | collective-permute-start | bytes 786440 | tf_op jit(solution)/shard_map/ppermute | solution.py:19
  10.7 49.9 %collective-permute-start.1 = (bf16[1,16,64,128]{3,2,1,0:T(8,128)(2,1)S(1)}, bf16[1,16,64,128]{3,2,1,0:T(8,128)(2,1)S(1)}, u32[]{:S(2)}, u32[]{:S(2)}) collective-permute-start(bf16[1,16,64,128]{3,2,1,0:T(8,128)(2,1)S(1)} %get-tuple-element.4), channel_id=1, source_target_pairs={{1,0},{2,1},{3,2},{4,3},{5,4},{6,5},{7,6},{8,7},{9,8},{10,9},{11,1... | collective-permute-start | bytes 786440 | tf_op jit(solution)/shard_map/ppermute | solution.py:21
  13.9 46.8 %copy-start.4 = (bf16[6,64,64]{2,1,0:T(8,128)(2,1)S(1)}, bf16[6,64,64]{2,1,0:T(8,128)(2,1)}, u32[]{:S(2)}) copy-start(bf16[6,64,64]{2,1,0:T(8,128)(2,1)} %param.16) | copy-start | bytes 147460
  13.9 50.1 %all-to-all-start = ((bf16[2,16,64,128]{3,2,0,1:T(8,128)(2,1)}), bf16[2,16,64,128]{3,2,0,1:T(8,128)(2,1)S(1)}, u32[]{:S(2)}, u32[]{:S(2)}) async-start(bf16[2,16,64,128]{3,2,0,1:T(8,128)(2,1)} %copy.40), calls=%async_computation | async-start | bytes 1048576 | tf_op jit(solution)/shard_map/all_to_all | solution.py:58
  67.4 20.5 %all-to-all-start.1 = ((bf16[32,1,64,128]{3,2,1,0:T(8,128)(2,1)}), bf16[32,1,64,128]{3,2,1,0:T(8,128)(2,1)S(1)}, u32[]{:S(2)}, u32[]{:S(2)}) async-start(bf16[32,1,64,128]{3,2,1,0:T(8,128)(2,1)} %copy.44), calls=%async_computation.1 | async-start | bytes 1048576 | tf_op jit(solution)/shard_map/all_to_all | solution.py:63
  74.2 2.9 %copy-start.3 = (f32[2,16,128,64]{2,3,1,0:T(8,128)S(1)}, f32[2,16,128,64]{2,3,1,0:T(8,128)}, u32[]{:S(2)}) copy-start(f32[2,16,128,64]{2,3,1,0:T(8,128)} %fusion.76) | copy-start | bytes 3145732
  74.2 2.9 %copy-start.12 = (bf16[64,64]{1,0:T(8,128)(2,1)S(1)}, bf16[64,64]{1,0:T(8,128)(2,1)}, u32[]{:S(2)}) copy-start(bf16[64,64]{1,0:T(8,128)(2,1)} %param.17) | copy-start | bytes 24580
  75.7 13.0 %copy-start.10 = (f32[64]{0:T(128)S(1)}, f32[64]{0:T(128)}, u32[]{:S(2)}) copy-start(f32[64]{0:T(128)} %param.19) | copy-start | bytes 772
  87.9 0.8 copy-start.2
  93.7 11.5 %collective-permute-start.2 = (bf16[1,16,64,128]{3,2,1,0:T(8,128)(2,1)S(1)}, bf16[1,16,64,128]{3,2,1,0:T(8,128)(2,1)S(1)}, u32[]{:S(2)}, u32[]{:S(2)}) collective-permute-start(bf16[1,16,64,128]{3,2,1,0:T(8,128)(2,1)S(1)} %get-tuple-element.2), channel_id=1, source_target_pairs={{0,1},{1,2},{2,3},{3,4},{4,5},{5,6},{6,7},{7,8},{8,9},{9,10},{10,1... | collective-permute-start | bytes 786440 | tf_op jit(solution)/shard_map/ppermute | solution.py:19
  95.7 9.6 %collective-permute-start.3 = (bf16[1,16,64,128]{3,2,1,0:T(8,128)(2,1)S(1)}, bf16[1,16,64,128]{3,2,1,0:T(8,128)(2,1)S(1)}, u32[]{:S(2)}, u32[]{:S(2)}) collective-permute-start(bf16[1,16,64,128]{3,2,1,0:T(8,128)(2,1)S(1)} %get-tuple-element.3), channel_id=1, source_target_pairs={{1,0},{2,1},{3,2},{4,3},{5,4},{6,5},{7,6},{8,7},{9,8},{10,9},{11,1... | collective-permute-start | bytes 786440 | tf_op jit(solution)/shard_map/ppermute | solution.py:21
  97.0 21.5 %all-to-all-start.2 = ((bf16[2,16,64,128]{3,2,0,1:T(8,128)(2,1)}), bf16[2,16,64,128]{3,2,0,1:T(8,128)(2,1)}, u32[]{:S(2)}, u32[]{:S(2)}) async-start(bf16[2,16,64,128]{3,2,0,1:T(8,128)(2,1)} %copy.49), calls=%async_computation.2 | async-start | bytes 1048576 | tf_op jit(solution)/shard_map/all_to_all | solution.py:58
  110.8 7.6 %copy-start.7 = (bf16[16,64]{0,1:T(8,128)(2,1)S(1)}, bf16[16,64]{0,1:T(8,128)(2,1)}, u32[]{:S(2)}) copy-start(bf16[16,64]{0,1:T(8,128)(2,1)} %copy.51) | copy-start | bytes 6148
  110.8 7.6 %copy-start.9 = (f32[32]{0:T(128)S(1)}, f32[32]{0:T(128)}, u32[]{:S(2)}) copy-start(f32[32]{0:T(128)} %multiply_add_fusion) | copy-start | bytes 388
  121.7 101.7 %all-to-all-start.3 = ((bf16[32,1,64,128]{3,2,1,0:T(8,128)(2,1)}), bf16[32,1,64,128]{3,2,1,0:T(8,128)(2,1)S(1)}, u32[]{:S(2)}, u32[]{:S(2)}) async-start(bf16[32,1,64,128]{3,2,1,0:T(8,128)(2,1)} %copy.55), calls=%async_computation.3 | async-start | bytes 1048576 | tf_op jit(solution)/shard_map/all_to_all | solution.py:63
  125.8 95.9 %all-reduce.6.cloned.1.call-start = ((), (), s32[]{:S(2)}) async-start(), calls=%async_computation.4 | async-start | bytes 393216 | tf_op jit(solution)/shard_map/psum | solution.py:152
  129.8 93.6 %copy-start.13 = (bf16[64,64]{1,0:T(8,128)(2,1)S(1)}, bf16[64,64]{1,0:T(8,128)(2,1)}, u32[]{:S(2)}) copy-start(bf16[64,64]{1,0:T(8,128)(2,1)} %param.17) | copy-start | bytes 24580
Sparse Core Ops, SparseCore 0:
  130.6 91.0 all-reduce.5
where the time goes:
time: 242 us; the launch traced here: 241 us
  waiting for transfers between devices  102 us (42%)
  between operations  48.2 us (20%)
  matrix products  43.7 us (18%)
  starting transfers between devices  33.4 us (14%)
  local copies, waits for them, and re-layouts  8.26 us (3%)
  other arithmetic  5.98 us (2%)
    psum x1, waiting for transfers between devices, per_device(): summed = lax.psum(local_grad, 'gx')  89 us
    all_to_all x2, starting transfers between devices, spectral(): lax.all_to_all(slab, 'gx', split_axis=1, concat_axis=0, tiled=True)  16.4 us
    dot_general x6, matrix products, per_device(): jnp.einsum('oc,xycz->xyoz', kernel_weight[tile], moved, preferred_element...  10.4 us
    all_to_all x2, starting transfers between devices, spectral(): return lax.all_to_all(result, 'gx', split_axis=0, concat_axis=1, tiled=True)  10.1 us
    dot_general x6, matrix products, per_device(): jnp.einsum('oc,xyoz->xycz', kernel_weight[tile], back_moved, preferred_el...  9.73 us
    all_to_all x2, waiting for transfers between devices, spectral(): return lax.all_to_all(result, 'gx', split_axis=0, concat_axis=1, tiled=True)  7.95 us
    dot_general x1, matrix products, per_device(): jnp.einsum('oc,xyoz->xycz', lap_weight, laplace_ext(ext_grad), preferred_...  7.47 us
    dot_general x6, matrix products, per_device(): jnp.einsum('xyoz,xycz->oc', back_moved, features, preferred_element_type=...  6.05 us
  transfers between devices with their start and end apart: 9, of which 3 were waited for; matrix products, arithmetic and copies ran while one was open for 14% of the time, Pallas kernels for 0%

commit v1 on v0

--- a/solution.py
+++ b/solution.py
@@ -1,3 +1,4 @@
+import functools
 from functools import partial
 import math
 import jax
@@ -6,6 +7,45 @@
 from jax.sharding import PartitionSpec as P
 
 RAD = 2
+
+
+def widths_tell(u, array_dim, sample):
+    view_out = u.shape
+    front = u.reshape(
+        *view_out[:array_dim], sample, view_out[array_dim] // sample, *view_out[array_dim + 1 :]
+    )
+    out_arr = jnp.moveaxis(front, array_dim, 0)
+    return out_arr
+
+
+def mix_the_chains(inputs, which_dim):
+    inputs = jnp.moveaxis(inputs, 0, which_dim)
+    last = inputs.shape
+    tmp = inputs.reshape(
+        *last[:which_dim], last[which_dim] * last[which_dim + 1], *last[which_dim + 2 :]
+    )
+    return tmp
+
+
+def _lead_stops_all(point, mesh_dim, base_x, values):
+    u_next, formed = (jax.lax.axis_size(mesh_dim), jax.lax.axis_index(mesh_dim))
+    reached = widths_tell(point, base_x, u_next)
+    dev_j = 1
+    parts_seen = [reached[formed]]
+    while dev_j < u_next:
+        current_value = reached[formed ^ dev_j]
+        parts_seen.append(
+            jax.lax.ppermute(
+                current_value, mesh_dim, perm=[(num, num ^ dev_j) for num in range(u_next)]
+            )
+        )
+        dev_j += 1
+    reached = jnp.stack(parts_seen, 0)[formed ^ jnp.arange(u_next)]
+    far_arr = mix_the_chains(reached, values)
+    return far_arr
+
+
+divide_the_threads = functools.partial(_lead_stops_all, mesh_dim="gx", base_x=1, values=0)
 
 
 def with_halo(cells, sides, width):
@@ -54,12 +94,7 @@
 
 
 def spectral(slab, spec_weight, kept_modes, adjoint):
-    result = pencil_work(
-        lax.all_to_all(slab, "gx", split_axis=1, concat_axis=0, tiled=True),
-        spec_weight,
-        kept_modes,
-        adjoint,
-    )
+    result = pencil_work(divide_the_threads(slab), spec_weight, kept_modes, adjoint)
     return lax.all_to_all(result, "gx", split_axis=0, concat_axis=1, tiled=True)
 
 

time: 242 us -> 270 us (1.12)
  starting transfers between devices: 33.4 us -> 61.3 us
  matrix products: 43.7 us -> 38.9 us
    ppermute x0 -> x30, starting transfers between devices: none -> 43 us  [_lead_stops_all(): jax.lax.ppermute(current_value, mesh_dim, perm=[(num, num ^ dev_j) for nu...]
    all_to_all x2 -> x0, starting transfers between devices: 16.4 us -> none  [spectral(): lax.all_to_all(slab, 'gx', split_axis=1, concat_axis=0, tiled=True)]
    ppermute x0 -> x30, waiting for transfers between devices: none -> 13.3 us  [_lead_stops_all(): jax.lax.ppermute(current_value, mesh_dim, perm=[(num, num ^ dev_j) for nu...]
    all_to_all x2 -> x0, waiting for transfers between devices: 4.71 us -> none  [spectral(): lax.all_to_all(slab, 'gx', split_axis=1, concat_axis=0, tiled=True)]
    psum x1, waiting for transfers between devices: 89 us -> 85.2 us  [per_device(): summed = lax.psum(local_grad, 'gx')]
    dot_general x6, matrix products: 6.05 us -> 2.34 us  [per_device(): jnp.einsum('xyoz,xycz->oc', back_moved, features, preferred_element_type=...]
    all_to_all x2, waiting for transfers between devices: 7.95 us -> 4.45 us  [spectral(): return lax.all_to_all(result, 'gx', split_axis=0, concat_axis=1, tiled=True)]
  transfers between devices with their start and end apart: 9 -> 37, of which waited for: 3 -> 10; matrix products, arithmetic and copies ran while one was open for 14% -> 13% of each run, Pallas kernels for 0% -> 0%
where the time goes in v1:
time: 270 us; the launch traced here: 269 us
  waiting for transfers between devices  103 us (38%)
  starting transfers between devices  61.3 us (23%)
  between operations  48.7 us (18%)
  matrix products  38.9 us (14%)
  local copies, waits for them, and re-layouts  10.6 us (4%)
  other arithmetic  6.13 us (2%)
    psum x1, waiting for transfers between devices, per_device(): summed = lax.psum(local_grad, 'gx')  85.2 us
    ppermute x30, starting transfers between devices, _lead_stops_all(): jax.lax.ppermute(current_value, mesh_dim, perm=[(num, num ^ dev_j) for nu...  43 us
    ppermute x30, waiting for transfers between devices, _lead_stops_all(): jax.lax.ppermute(current_value, mesh_dim, perm=[(num, num ^ dev_j) for nu...  13.3 us
    all_to_all x2, starting transfers between devices, spectral(): return lax.all_to_all(result, 'gx', split_axis=0, concat_axis=1, tiled=True)  10.8 us
    dot_general x6, matrix products, per_device(): jnp.einsum('oc,xycz->xyoz', kernel_weight[tile], moved, preferred_element...  10.4 us
    dot_general x6, matrix products, per_device(): jnp.einsum('oc,xyoz->xycz', kernel_weight[tile], back_moved, preferred_el...  9.76 us
    dot_general x1, matrix products, per_device(): jnp.einsum('oc,xyoz->xycz', lap_weight, laplace_ext(ext_grad), preferred_...  7.87 us
  transfers between devices with their start and end apart: 37, of which 10 were waited for; matrix products, arithmetic and copies ran while one was open for 13% of the time, Pallas kernels for 0%

profile of v1, /device:TPU:0, one launch (start us, length us, event | category | flops | bytes accessed | tf_op | source)
XLA Modules:
  0.0 268.6 jit_solution(2034876682013506445)
XLA Ops:
  9.0 2.6 collective-permute-start.3
  16.0 2.0 fusion.150
  54.2 2.7 %collective-permute-start.7 = (bf16[2,1,64,128]{3,2,0,1:T(8,128)(2,1)S(1)}, bf16[2,1,64,128]{3,2,0,1:T(8,128)(2,1)S(1)}, u32[]{:S(2)}, u32[]{:S(2)}) collective-permute-start(bf16[2,1,64,128]{3,2,0,1:T(8,128)(2,1)S(1)} %get-tuple-element.29), channel_id=1, source_target_pairs={{0,6},{1,7},{2,4},{3,5},{4,2},{5,3},{6,0},{7,1},{8,14},{9,15},{10,... | collective-permute-start | bytes 98312 | tf_op jit(solution)/shard_map/ppermute | solution.py:38
  57.1 2.8 %collective-permute-start.9 = (bf16[2,1,64,128]{3,2,0,1:T(8,128)(2,1)S(1)}, bf16[2,1,64,128]{3,2,0,1:T(8,128)(2,1)S(1)}, u32[]{:S(2)}, u32[]{:S(2)}) collective-permute-start(bf16[2,1,64,128]{3,2,0,1:T(8,128)(2,1)S(1)} %get-tuple-element.27), channel_id=1, source_target_pairs={{0,8},{1,9},{2,10},{3,11},{4,12},{5,13},{6,14},{7,15},{8,0},{9,1},... | collective-permute-start | bytes 98312 | tf_op jit(solution)/shard_map/ppermute | solution.py:38
  60.0 3.6 %collective-permute-start.11 = (bf16[2,1,64,128]{3,2,0,1:T(8,128)(2,1)S(1)}, bf16[2,1,64,128]{3,2,0,1:T(8,128)(2,1)S(1)}, u32[]{:S(2)}, u32[]{:S(2)}) collective-permute-start(bf16[2,1,64,128]{3,2,0,1:T(8,128)(2,1)S(1)} %get-tuple-element.25), channel_id=1, source_target_pairs={{0,10},{1,11},{2,8},{3,9},{4,14},{5,15},{6,12},{7,13},{8,2},{9,3},... | collective-permute-start | bytes 98312 | tf_op jit(solution)/shard_map/ppermute | solution.py:38
  63.7 3.6 %collective-permute-start.13 = (bf16[2,1,64,128]{3,2,0,1:T(8,128)(2,1)S(1)}, bf16[2,1,64,128]{3,2,0,1:T(8,128)(2,1)S(1)}, u32[]{:S(2)}, u32[]{:S(2)}) collective-permute-start(bf16[2,1,64,128]{3,2,0,1:T(8,128)(2,1)S(1)} %get-tuple-element.23), channel_id=1, source_target_pairs={{0,12},{1,13},{2,14},{3,15},{4,8},{5,9},{6,10},{7,11},{8,4},{9,5},... | collective-permute-start | bytes 98312 | tf_op jit(solution)/shard_map/ppermute | solution.py:38
  67.5 4.5 %collective-permute-start.15 = (bf16[2,1,64,128]{3,2,0,1:T(8,128)(2,1)S(1)}, bf16[2,1,64,128]{3,2,0,1:T(8,128)(2,1)S(1)}, u32[]{:S(2)}, u32[]{:S(2)}) collective-permute-start(bf16[2,1,64,128]{3,2,0,1:T(8,128)(2,1)S(1)} %get-tuple-element.35), channel_id=1, source_target_pairs={{0,14},{1,15},{2,12},{3,13},{4,10},{5,11},{6,8},{7,9},{8,6},{9,7},... | collective-permute-start | bytes 98312 | tf_op jit(solution)/shard_map/ppermute | solution.py:38
  72.1 2.2 collective-permute-start
  75.8 2.3 collective-permute-done.16
  80.9 5.6 %all-to-all-start = ((bf16[32,1,64,128]{3,2,1,0:T(8,128)(2,1)}), bf16[32,1,64,128]{3,2,1,0:T(8,128)(2,1)S(1)}, u32[]{:S(2)}, u32[]{:S(2)}) async-start(bf16[32,1,64,128]{3,2,1,0:T(8,128)(2,1)} %copy.111), calls=%async_computation | async-start | bytes 1048576 | tf_op jit(solution)/shard_map/all_to_all | solution.py:98
  93.6 2.9 %convolution_add_fusion.1 = f32[2,16,128,64]{2,3,1,0:T(8,128)} fusion(f32[2,16,128,64]{2,3,1,0:T(8,128)S(1)} %copy-done.3, f32[4,18,64,130]{3,2,1,0:T(8,128)S(1)} %pad_convert_fusion.1, bf16[64,64]{1,0:T(8,128)(2,1)S(1)} %copy-done.8), kind=kOutput, calls=%fused_computation.39 | convolution fusion | flops 35913728 | bytes 9453568 | tf_op jit(solution)/shard_map/oc,xycz->xyoz/dot_general | solution.py:152
  96.5 4.4 %all-to-all-done = bf16[32,1,64,128]{3,2,1,0:T(8,128)(2,1)S(1)} async-done(((bf16[32,1,64,128]{3,2,1,0:T(8,128)(2,1)}), bf16[32,1,64,128]{3,2,1,0:T(8,128)(2,1)S(1)}, u32[]{:S(2)}, u32[]{:S(2)}) %all-to-all-start) | async-done | bytes 524320 | tf_op jit(solution)/shard_map/all_to_all | solution.py:98
  101.7 4.2 %fusion.33 = bf16[2,16,64,128]{3,2,1,0:T(8,128)(2,1)S(1)} fusion(bf16[2,16,64,128]{3,2,1,0:T(8,128)(2,1)} %param.11, f32[2,16,128,64]{2,3,1,0:T(8,128)} %fusion.51, f32[2,16,128,64]{2,3,1,0:T(8,128)} %fusion.50, f32[2,16,128,64]{2,3,1,0:T(8,128)} %fusion.49, f32[2,16,128,64]{2,3,1,0:T(8,128)} %fusion.48, f32[2,16,128,64]{2,3,1,0:T(8,128)S(1)} %fusion.47, ...), kind=kOutput, calls=%fused_computation.74 | convolution fusion | flops 41680896 | bytes 8945932 | tf_op jit(solution)/shard_map/oc,xycz->xyoz/dot_general | solution.py:157
  107.5 2.4 collective-permute-start.17
  111.4 3.1 %collective-permute-start.20 = (bf16[2,1,64,128]{3,2,0,1:T(8,128)(2,1)S(1)}, bf16[2,1,64,128]{3,2,0,1:T(8,128)(2,1)S(1)}, u32[]{:S(2)}, u32[]{:S(2)}) collective-permute-start(bf16[2,1,64,128]{3,2,0,1:T(8,128)(2,1)S(1)} %get-tuple-element.14), channel_id=1, source_target_pairs={{0,2},{1,3},{2,0},{3,1},{4,6},{5,7},{6,4},{7,5},{8,10},{9,11},{10,... | collective-permute-start | bytes 98312 | tf_op jit(solution)/shard_map/ppermute | solution.py:38
  116.2 3.5 %collective-permute-done.20 = bf16[2,1,64,128]{3,2,0,1:T(8,128)(2,1)S(1)} collective-permute-done((bf16[2,1,64,128]{3,2,0,1:T(8,128)(2,1)S(1)}, bf16[2,1,64,128]{3,2,0,1:T(8,128)(2,1)S(1)}, u32[]{:S(2)}, u32[]{:S(2)}) %collective-permute-start.20) | collective-permute-done | bytes 32800 | tf_op jit(solution)/shard_map/ppermute | solution.py:38
  119.7 3.2 %collective-permute-start.24 = (bf16[2,1,64,128]{3,2,0,1:T(8,128)(2,1)S(1)}, bf16[2,1,64,128]{3,2,0,1:T(8,128)(2,1)S(1)}, u32[]{:S(2)}, u32[]{:S(2)}) collective-permute-start(bf16[2,1,64,128]{3,2,0,1:T(8,128)(2,1)S(1)} %get-tuple-element.10), channel_id=1, source_target_pairs={{0,6},{1,7},{2,4},{3,5},{4,2},{5,3},{6,0},{7,1},{8,14},{9,15},{10,... | collective-permute-start | bytes 98312 | tf_op jit(solution)/shard_map/ppermute | solution.py:38
  136.7 3.0 %collective-permute-start.33 = (bf16[2,1,64,128]{3,2,1,0:T(8,128)(2,1)S(1)}, bf16[2,1,64,128]{3,2,1,0:T(8,128)(2,1)S(1)}, u32[]{:S(2)}, u32[]{:S(2)}) collective-permute-start(bf16[2,1,64,128]{3,2,1,0:T(8,128)(2,1)S(1)} %get-tuple-element.2), channel_id=1, source_target_pairs={{0,15},{1,14},{2,13},{3,12},{4,11},{5,10},{6,9},{7,8},{8,7},{9,6},... | collective-permute-start | bytes 98312 | tf_op jit(solution)/shard_map/ppermute | solution.py:38
  139.7 2.6 collective-permute-done.32
  145.7 5.2 %all-to-all-start.1 = ((bf16[32,1,64,128]{3,2,1,0:T(8,128)(2,1)}), bf16[32,1,64,128]{3,2,1,0:T(8,128)(2,1)}, u32[]{:S(2)}, u32[]{:S(2)}) async-start(bf16[32,1,64,128]{3,2,1,0:T(8,128)(2,1)} %copy.135), calls=%async_computation.1 | async-start | bytes 1048576 | tf_op jit(solution)/shard_map/all_to_all | solution.py:98
  160.5 2.9 %pad_convert_fusion = f32[4,18,64,130]{3,2,1,0:T(8,128)} fusion(bf16[4,16,64,128]{3,2,1,0:T(8,128)(2,1)S(1)} %pad_maximum_fusion), kind=kLoop, calls=%fused_computation.14 | loop fusion | flops 599040 | bytes 3444736 | tf_op jit(solution)/shard_map/convert_element_type | solution.py:102
  163.4 85.2 %all-reduce.6.cloned.1.call-done = f32[6,64,64]{2,1,0:T(8,128)} async-done(((f32[6,64,64]{2,1,0:T(8,128)}), f32[6,64,64]{2,1,0:T(8,128)}) %all-reduce.6.cloned.1.call-update) | async-done | bytes 98320 | tf_op jit(solution)/shard_map/psum | solution.py:187
  250.3 7.9 %fusion.15 = f32[2,16,64,128]{3,2,1,0:T(8,128)S(1)} fusion(f32[2,16,128,64]{2,3,1,0:T(8,128)} %fusion.74, f32[4,18,64,130]{3,2,1,0:T(8,128)} %pad_convert_fusion, bf16[64,64]{1,0:T(8,128)(2,1)S(1)} %copy-done.9, bf16[16,2,1,64,128]{4,3,1,0,2:T(8,128)(2,1)} %bitcast.201), kind=kOutput, calls=%fused_computation.42 | convolution fusion | flops 36438016 | bytes 9969664 | tf_op jit(solution)/shard_map/oc,xyoz->xycz/dot_general | solution.py:170
  258.2 3.5 %fusion.16 = bf16[2,16,64,128]{3,2,1,0:T(8,128)(2,1)} fusion(f32[2,16,64,128]{3,2,1,0:T(8,128)} %convolution_bitcast_fusion, f32[2,16,64,128]{3,2,1,0:T(8,128)} %convolution_bitcast_fusion.1, f32[2,16,64,128]{3,2,1,0:T(8,128)} %convolution_bitcast_fusion.2, f32[2,16,64,128]{3,2,1,0:T(8,128)S(1)} %convolution_bitcast_fusion.3, ...), kind=kOutput, calls=%fused_computation.45 | convolution fusion | flops 35389440 | bytes 7880716 | tf_op jit(solution)/shard_map/oc,xyoz->xycz/dot_general | solution.py:177
  (154 shorter events, 54.0 us)
Async XLA Ops:
  8.5 45.7 %collective-permute-start.2 = (bf16[2,1,64,128]{3,2,0,1:T(8,128)(2,1)S(1)}, bf16[2,1,64,128]{3,2,0,1:T(8,128)(2,1)S(1)}, u32[]{:S(2)}, u32[]{:S(2)}) collective-permute-start(bf16[2,1,64,128]{3,2,0,1:T(8,128)(2,1)S(1)} %get-tuple-element.34), channel_id=1, source_target_pairs={{0,1},{1,0},{2,3},{3,2},{4,5},{5,4},{6,7},{7,6},{8,9},{9,8},{10,11... | collective-permute-start | bytes 98312 | tf_op jit(solution)/shard_map/ppermute | solution.py:38
  9.0 47.9 %collective-permute-start.3 = (bf16[2,1,64,128]{3,2,0,1:T(8,128)(2,1)S(1)}, bf16[2,1,64,128]{3,2,0,1:T(8,128)(2,1)S(1)}, u32[]{:S(2)}, u32[]{:S(2)}) collective-permute-start(bf16[2,1,64,128]{3,2,0,1:T(8,128)(2,1)S(1)} %get-tuple-element.33), channel_id=1, source_target_pairs={{0,2},{1,3},{2,0},{3,1},{4,6},{5,7},{6,4},{7,5},{8,10},{9,11},{10,... | collective-permute-start | bytes 98312 | tf_op jit(solution)/shard_map/ppermute | solution.py:38
  11.6 45.5 %collective-permute-start.4 = (bf16[2,1,64,128]{3,2,0,1:T(8,128)(2,1)S(1)}, bf16[2,1,64,128]{3,2,0,1:T(8,128)(2,1)S(1)}, u32[]{:S(2)}, u32[]{:S(2)}) collective-permute-start(bf16[2,1,64,128]{3,2,0,1:T(8,128)(2,1)S(1)} %get-tuple-element.32), channel_id=1, source_target_pairs={{0,3},{1,2},{2,1},{3,0},{4,7},{5,6},{6,5},{7,4},{8,11},{9,10},{10,... | collective-permute-start | bytes 98312 | tf_op jit(solution)/shard_map/ppermute | solution.py:38
  11.7 48.2 %collective-permute-start.5 = (bf16[2,1,64,128]{3,2,0,1:T(8,128)(2,1)S(1)}, bf16[2,1,64,128]{3,2,0,1:T(8,128)(2,1)S(1)}, u32[]{:S(2)}, u32[]{:S(2)}) collective-permute-start(bf16[2,1,64,128]{3,2,0,1:T(8,128)(2,1)S(1)} %get-tuple-element.31), channel_id=1, source_target_pairs={{0,4},{1,5},{2,6},{3,7},{4,0},{5,1},{6,2},{7,3},{8,12},{9,13},{10,... | collective-permute-start | bytes 98312 | tf_op jit(solution)/shard_map/ppermute | solution.py:38
  13.5 46.5 %collective-permute-start.6 = (bf16[2,1,64,128]{3,2,0,1:T(8,128)(2,1)S(1)}, bf16[2,1,64,128]{3,2,0,1:T(8,128)(2,1)S(1)}, u32[]{:S(2)}, u32[]{:S(2)}) collective-permute-start(bf16[2,1,64,128]{3,2,0,1:T(8,128)(2,1)S(1)} %get-tuple-element.30), channel_id=1, source_target_pairs={{0,5},{1,4},{2,7},{3,6},{4,1},{5,0},{6,3},{7,2},{8,13},{9,12},{10,... | collective-permute-start | bytes 98312 | tf_op jit(solution)/shard_map/ppermute | solution.py:38
  54.2 9.3 %collective-permute-start.7 = (bf16[2,1,64,128]{3,2,0,1:T(8,128)(2,1)S(1)}, bf16[2,1,64,128]{3,2,0,1:T(8,128)(2,1)S(1)}, u32[]{:S(2)}, u32[]{:S(2)}) collective-permute-start(bf16[2,1,64,128]{3,2,0,1:T(8,128)(2,1)S(1)} %get-tuple-element.29), channel_id=1, source_target_pairs={{0,6},{1,7},{2,4},{3,5},{4,2},{5,3},{6,0},{7,1},{8,14},{9,15},{10,... | collective-permute-start | bytes 98312 | tf_op jit(solution)/shard_map/ppermute | solution.py:38
  56.9 6.8 %collective-permute-start.8 = (bf16[2,1,64,128]{3,2,0,1:T(8,128)(2,1)S(1)}, bf16[2,1,64,128]{3,2,0,1:T(8,128)(2,1)S(1)}, u32[]{:S(2)}, u32[]{:S(2)}) collective-permute-start(bf16[2,1,64,128]{3,2,0,1:T(8,128)(2,1)S(1)} %get-tuple-element.28), channel_id=1, source_target_pairs={{0,7},{1,6},{2,5},{3,4},{4,3},{5,2},{6,1},{7,0},{8,15},{9,14},{10,... | collective-permute-start | bytes 98312 | tf_op jit(solution)/shard_map/ppermute | solution.py:38
  57.1 10.3 %collective-permute-start.9 = (bf16[2,1,64,128]{3,2,0,1:T(8,128)(2,1)S(1)}, bf16[2,1,64,128]{3,2,0,1:T(8,128)(2,1)S(1)}, u32[]{:S(2)}, u32[]{:S(2)}) collective-permute-start(bf16[2,1,64,128]{3,2,0,1:T(8,128)(2,1)S(1)} %get-tuple-element.27), channel_id=1, source_target_pairs={{0,8},{1,9},{2,10},{3,11},{4,12},{5,13},{6,14},{7,15},{8,0},{9,1},... | collective-permute-start | bytes 98312 | tf_op jit(solution)/shard_map/ppermute | solution.py:38
  59.9 7.6 %collective-permute-start.10 = (bf16[2,1,64,128]{3,2,0,1:T(8,128)(2,1)S(1)}, bf16[2,1,64,128]{3,2,0,1:T(8,128)(2,1)S(1)}, u32[]{:S(2)}, u32[]{:S(2)}) collective-permute-start(bf16[2,1,64,128]{3,2,0,1:T(8,128)(2,1)S(1)} %get-tuple-element.26), channel_id=1, source_target_pairs={{0,9},{1,8},{2,11},{3,10},{4,13},{5,12},{6,15},{7,14},{8,1},{9,0},... | collective-permute-start | bytes 98312 | tf_op jit(solution)/shard_map/ppermute | solution.py:38
  60.0 12.0 %collective-permute-start.11 = (bf16[2,1,64,128]{3,2,0,1:T(8,128)(2,1)S(1)}, bf16[2,1,64,128]{3,2,0,1:T(8,128)(2,1)S(1)}, u32[]{:S(2)}, u32[]{:S(2)}) collective-permute-start(bf16[2,1,64,128]{3,2,0,1:T(8,128)(2,1)S(1)} %get-tuple-element.25), channel_id=1, source_target_pairs={{0,10},{1,11},{2,8},{3,9},{4,14},{5,15},{6,12},{7,13},{8,2},{9,3},... | collective-permute-start | bytes 98312 | tf_op jit(solution)/shard_map/ppermute | solution.py:38
  63.6 8.6 %collective-permute-start.12 = (bf16[2,1,64,128]{3,2,0,1:T(8,128)(2,1)S(1)}, bf16[2,1,64,128]{3,2,0,1:T(8,128)(2,1)S(1)}, u32[]{:S(2)}, u32[]{:S(2)}) collective-permute-start(bf16[2,1,64,128]{3,2,0,1:T(8,128)(2,1)S(1)} %get-tuple-element.24), channel_id=1, source_target_pairs={{0,11},{1,10},{2,9},{3,8},{4,15},{5,14},{6,13},{7,12},{8,3},{9,2},... | collective-permute-start | bytes 98312 | tf_op jit(solution)/shard_map/ppermute | solution.py:38
  63.7 10.7 %collective-permute-start.13 = (bf16[2,1,64,128]{3,2,0,1:T(8,128)(2,1)S(1)}, bf16[2,1,64,128]{3,2,0,1:T(8,128)(2,1)S(1)}, u32[]{:S(2)}, u32[]{:S(2)}) collective-permute-start(bf16[2,1,64,128]{3,2,0,1:T(8,128)(2,1)S(1)} %get-tuple-element.23), channel_id=1, source_target_pairs={{0,12},{1,13},{2,14},{3,15},{4,8},{5,9},{6,10},{7,11},{8,4},{9,5},... | collective-permute-start | bytes 98312 | tf_op jit(solution)/shard_map/ppermute | solution.py:38
  67.4 8.4 %collective-permute-start.14 = (bf16[2,1,64,128]{3,2,0,1:T(8,128)(2,1)S(1)}, bf16[2,1,64,128]{3,2,0,1:T(8,128)(2,1)S(1)}, u32[]{:S(2)}, u32[]{:S(2)}) collective-permute-start(bf16[2,1,64,128]{3,2,0,1:T(8,128)(2,1)S(1)} %get-tuple-element.22), channel_id=1, source_target_pairs={{0,13},{1,12},{2,15},{3,14},{4,9},{5,8},{6,11},{7,10},{8,5},{9,4},... | collective-permute-start | bytes 98312 | tf_op jit(solution)/shard_map/ppermute | solution.py:38
  67.5 8.3 %collective-permute-start.15 = (bf16[2,1,64,128]{3,2,0,1:T(8,128)(2,1)S(1)}, bf16[2,1,64,128]{3,2,0,1:T(8,128)(2,1)S(1)}, u32[]{:S(2)}, u32[]{:S(2)}) collective-permute-start(bf16[2,1,64,128]{3,2,0,1:T(8,128)(2,1)S(1)} %get-tuple-element.35), channel_id=1, source_target_pairs={{0,14},{1,15},{2,12},{3,13},{4,10},{5,11},{6,8},{7,9},{8,6},{9,7},... | collective-permute-start | bytes 98312 | tf_op jit(solution)/shard_map/ppermute | solution.py:38
  72.1 14.3 %collective-permute-start = (bf16[1,16,64,128]{3,2,1,0:T(8,128)(2,1)S(1)}, bf16[1,16,64,128]{3,2,1,0:T(8,128)(2,1)S(1)}, u32[]{:S(2)}, u32[]{:S(2)}) collective-permute-start(bf16[1,16,64,128]{3,2,1,0:T(8,128)(2,1)S(1)} %get-tuple-element.20), channel_id=1, source_target_pairs={{0,1},{1,2},{2,3},{3,4},{4,5},{5,6},{6,7},{7,8},{8,9},{9,10},{10,1... | collective-permute-start | bytes 786440 | tf_op jit(solution)/shard_map/ppermute | solution.py:59
  74.4 12.2 %collective-permute-start.1 = (bf16[1,16,64,128]{3,2,1,0:T(8,128)(2,1)S(1)}, bf16[1,16,64,128]{3,2,1,0:T(8,128)(2,1)S(1)}, u32[]{:S(2)}, u32[]{:S(2)}) collective-permute-start(bf16[1,16,64,128]{3,2,1,0:T(8,128)(2,1)S(1)} %get-tuple-element.19), channel_id=1, source_target_pairs={{1,0},{2,1},{3,2},{4,3},{5,4},{6,5},{7,6},{8,7},{9,8},{10,9},{11,1... | collective-permute-start | bytes 786440 | tf_op jit(solution)/shard_map/ppermute | solution.py:61
  80.9 20.0 %all-to-all-start = ((bf16[32,1,64,128]{3,2,1,0:T(8,128)(2,1)}), bf16[32,1,64,128]{3,2,1,0:T(8,128)(2,1)S(1)}, u32[]{:S(2)}, u32[]{:S(2)}) async-start(bf16[32,1,64,128]{3,2,1,0:T(8,128)(2,1)} %copy.111), calls=%async_computation | async-start | bytes 1048576 | tf_op jit(solution)/shard_map/all_to_all | solution.py:98
  107.5 7.1 %collective-permute-start.19 = (bf16[2,1,64,128]{3,2,0,1:T(8,128)(2,1)S(1)}, bf16[2,1,64,128]{3,2,0,1:T(8,128)(2,1)S(1)}, u32[]{:S(2)}, u32[]{:S(2)}) collective-permute-start(bf16[2,1,64,128]{3,2,0,1:T(8,128)(2,1)S(1)} %get-tuple-element.15), channel_id=1, source_target_pairs={{0,1},{1,0},{2,3},{3,2},{4,5},{5,4},{6,7},{7,6},{8,9},{9,8},{10,11... | collective-permute-start | bytes 98312 | tf_op jit(solution)/shard_map/ppermute | solution.py:38
  107.5 43.5 %collective-permute-start.17 = (bf16[1,16,64,128]{3,2,1,0:T(8,128)(2,1)S(1)}, bf16[1,16,64,128]{3,2,1,0:T(8,128)(2,1)S(1)}, u32[]{:S(2)}, u32[]{:S(2)}) collective-permute-start(bf16[1,16,64,128]{3,2,1,0:T(8,128)(2,1)S(1)} %get-tuple-element.17), channel_id=1, source_target_pairs={{0,1},{1,2},{2,3},{3,4},{4,5},{5,6},{6,7},{7,8},{8,9},{9,10},{10,1... | collective-permute-start | bytes 786440 | tf_op jit(solution)/shard_map/ppermute | solution.py:59
  110.0 41.1 %collective-permute-start.18 = (bf16[1,16,64,128]{3,2,1,0:T(8,128)(2,1)S(1)}, bf16[1,16,64,128]{3,2,1,0:T(8,128)(2,1)S(1)}, u32[]{:S(2)}, u32[]{:S(2)}) collective-permute-start(bf16[1,16,64,128]{3,2,1,0:T(8,128)(2,1)S(1)} %get-tuple-element.18), channel_id=1, source_target_pairs={{1,0},{2,1},{3,2},{4,3},{5,4},{6,5},{7,6},{8,7},{9,8},{10,9},{11,1... | collective-permute-start | bytes 786440 | tf_op jit(solution)/shard_map/ppermute | solution.py:61
  111.4 8.2 %collective-permute-start.20 = (bf16[2,1,64,128]{3,2,0,1:T(8,128)(2,1)S(1)}, bf16[2,1,64,128]{3,2,0,1:T(8,128)(2,1)S(1)}, u32[]{:S(2)}, u32[]{:S(2)}) collective-permute-start(bf16[2,1,64,128]{3,2,0,1:T(8,128)(2,1)S(1)} %get-tuple-element.14), channel_id=1, source_target_pairs={{0,2},{1,3},{2,0},{3,1},{4,6},{5,7},{6,4},{7,5},{8,10},{9,11},{10,... | collective-permute-start | bytes 98312 | tf_op jit(solution)/shard_map/ppermute | solution.py:38
  114.6 8.2 %collective-permute-start.22 = (bf16[2,1,64,128]{3,2,0,1:T(8,128)(2,1)S(1)}, bf16[2,1,64,128]{3,2,0,1:T(8,128)(2,1)S(1)}, u32[]{:S(2)}, u32[]{:S(2)}) collective-permute-start(bf16[2,1,64,128]{3,2,0,1:T(8,128)(2,1)S(1)} %get-tuple-element.12), channel_id=1, source_target_pairs={{0,4},{1,5},{2,6},{3,7},{4,0},{5,1},{6,2},{7,3},{8,12},{9,13},{10,... | collective-permute-start | bytes 98312 | tf_op jit(solution)/shard_map/ppermute | solution.py:38
  145.7 104.6 %all-to-all-start.1 = ((bf16[32,1,64,128]{3,2,1,0:T(8,128)(2,1)}), bf16[32,1,64,128]{3,2,1,0:T(8,128)(2,1)}, u32[]{:S(2)}, u32[]{:S(2)}) async-start(bf16[32,1,64,128]{3,2,1,0:T(8,128)(2,1)} %copy.135), calls=%async_computation.1 | async-start | bytes 1048576 | tf_op jit(solution)/shard_map/all_to_all | solution.py:98
  151.0 97.7 %all-reduce.6.cloned.1.call-start = ((), (), s32[]{:S(2)}) async-start(), calls=%async_computation.2 | async-start | bytes 393216 | tf_op jit(solution)/shard_map/psum | solution.py:187
  (23 other events, 278.4 us)
Sparse Core Ops, SparseCore 0:
  157.7 90.9 all-reduce.5
